TPU v7x, 512 devices: a whole 4x4x16 slice. The times are simulated.
512 devices in a mesh: fib: 16 (over y, x), blk: 32 (over z, core).
Axes of the slice: x: 4, y: 4, z: 16, core: 2. Of those that a mesh axis runs over, the one named last changes fastest.
Arguments:
- field_data: float32 [33, 64, 512, 256], P(None, 'blk', 'fib'), may hold values from -120 to 120
- start_block: float32 [512, 64], replicated, may hold values from -6 to 6
Outputs:
- core_out: float32 [33, 64, 64, 256], P(None, 'blk', 'fib')
All inputs are finite; a program needn't handle non-finite values.
Results may differ from a plain program's by a relative error of at most 0.00013.
Values sent between devices are 32-bit elements; how exact they have to be, the bound alone decides.
A program may use at most 192 MiB of HBM per device.

v0:
```python
import jax
import jax.numpy as jnp
from jax import lax
from jax.sharding import PartitionSpec as P


def shards(field_data, start_block):
    highest = lax.Precision.HIGHEST
    received = lax.all_to_all(field_data, "fib", split_axis=3, concat_axis=2, tiled=True)
    width_x = received.shape[2]
    unfolded = jnp.transpose(received, (0, 1, 3, 2)).reshape(-1, width_x)
    contract_rows = (((0,), (0,)), ((), ()))
    local_gram = lax.dot_general(unfolded, unfolded, contract_rows, precision=highest)
    gram_total = lax.psum(local_gram, ("fib", "blk"))
    raw_basis = jnp.dot(gram_total, start_block, precision=highest)
    inner_block = jnp.dot(raw_basis.T, raw_basis, precision=highest)
    lower_factor = jnp.linalg.cholesky(inner_block)
    basis_cols = jax.scipy.linalg.solve_triangular(lower_factor, raw_basis.T, lower=True).T
    core_local = jnp.einsum("szxy,xr->szry", received, basis_cols, precision=highest)
    return lax.all_to_all(core_local, "fib", split_axis=2, concat_axis=3, tiled=True)


def solution(mesh):
    in_specs = (P(None, "blk", "fib", None), P())
    out_specs = P(None, "blk", "fib", None)
    return jax.shard_map(shards, mesh=mesh, in_specs=in_specs, out_specs=out_specs, check_vma=False)
```

profile of v0, /device:TPU:1, one launch (start us, length us, event | category | flops | bytes accessed | tf_op | source)
XLA Modules:
  0.0 619.4 jit_solution(7491580162648552195)
XLA Ops:
  6.5 0.0 copy-start
  6.5 0.0 all-reduce.2.cloned.1.call-start
  6.5 8.7 %copy.13 = f32[33,2,32,256]{0,2,1,3:T(8,128)} copy(f32[33,2,32,256]{3,2,1,0:T(8,128)} %param.2) | data formatting | bytes 4325376 | tf_op args[0]
  15.2 10.1 %reshape.13 = f32[16,1,33792]{2,1,0:T(1,128)S(1)} reshape(f32[256,2,32,33]{3,2,1,0:T(8,128)} %bitcast.45) | data formatting | bytes 4325376
  25.3 34.1 %all_to_all.36 = f32[16,1,33792]{2,1,0:T(1,128)} all-to-all(f32[16,1,33792]{2,1,0:T(1,128)S(1)} %reshape.13), channel_id=1, replica_groups=mesh['fib'=16,'blk'=32] {'fib'}, dimensions={0} | all-to-all | bytes 4325376 | tf_op jit(solution)/shard_map/all_to_all | solution.py:9
  59.4 0.5 broadcast.53
  59.9 7.4 %reduce.6 = f32[16,33792]{1,0:T(8,128)S(1)} reduce(f32[16,1,33792]{2,1,0:T(1,128)} %all_to_all.36, f32[]{:T(128)} %broadcast.53), dimensions={1}, to_apply=%all_to_all.26.reduce_sub_computation | reduce | bytes 4325380 | tf_op jit(solution)/shard_map/all_to_all | solution.py:9
  67.3 12.4 %reshape.14 = f32[256,2,32,33]{3,2,1,0:T(8,128)} reshape(f32[16,33792]{1,0:T(8,128)S(1)} %reduce.6) | data formatting | bytes 4325376
  79.8 11.7 %copy.15 = f32[33,2,16,32,16]{3,2,4,1,0:T(8,128)} copy(f32[33,2,16,32,16]{0,3,1,4,2:T(8,128)} %bitcast.46) | data formatting | bytes 4325376 | tf_op jit(solution)/shard_map/all_to_all | solution.py:9
  91.5 6.7 %all_to_all.29 = f32[33,2,512,16]{2,3,1,0:T(8,128)S(1)} reshape(f32[33,2,16,32,16]{3,2,4,1,0:T(8,128)} %copy.15) | data formatting | bytes 4325376 | tf_op jit(solution)/shard_map/all_to_all | solution.py:9
  98.2 5.4 fusion.4
  103.5 0.0 all-reduce.2.cloned.1.call-update
  103.6 470.4 %all-reduce.2.cloned.1.call-done = f32[512,512]{1,0:T(8,128)} async-done(((f32[512,512]{1,0:T(8,128)}), f32[512,512]{1,0:T(8,128)}) %all-reduce.2.cloned.1.call-update) | async-done | bytes 1048592 | tf_op jit(solution)/shard_map/psum | solution.py:14
  574.0 0.0 copy-done
  574.0 2.4 fusion.13
  576.4 0.3 fusion.14
  576.6 0.1 copy.16
  576.7 5.8 cholesky.16
  582.6 0.7 compare_reduce_fusion
  583.3 0.7 fusion.10
  584.0 4.9 custom-call.7
  588.9 0.3 convolution_bitcast_fusion
  589.3 3.0 fusion.7
  592.3 1.0 copy.18
  593.3 1.0 reshape.15
  594.3 14.6 %all_to_all.37 = f32[16,1,4224]{2,1,0:T(1,128)S(1)} all-to-all(f32[16,1,4224]{2,1,0:T(1,128)S(1)} %reshape.15), channel_id=1, replica_groups=mesh['fib'=16,'blk'=32] {'fib'}, dimensions={0} | all-to-all | bytes 540672 | tf_op jit(solution)/shard_map/all_to_all | solution.py:20
  608.9 1.3 reduce.7
  610.2 1.1 reshape.16
  611.4 0.1 copy.20
  611.5 1.0 copy.21
  (2 shorter events, 0.0 us)
Async XLA Ops:
  6.5 567.5 %copy-start = (f32[512,64]{0,1:T(8,128)S(1)}, f32[512,64]{0,1:T(8,128)}, u32[]{:S(2)}) copy-start(f32[512,64]{0,1:T(8,128)} %param.3) | copy-start | bytes 393220
  6.5 567.5 %all-reduce.2.cloned.1.call-start = ((), (), s32[]{:S(2)}) async-start(), calls=%async_computation.2 | async-start | bytes 2097152 | tf_op jit(solution)/shard_map/psum | solution.py:14
Sparse Core Ops, SparseCore 0:
  103.7 470.2 all-reduce.1
where the time goes:
time: 620 us; the launch traced here: 619 us
  waiting for transfers between devices  470 us (76%)
  local copies, waits for them, and re-layouts  54.5 us (9%)
  blocking collectives  48.7 us (8%)
  other arithmetic  20.9 us (3%)
  between operations  13.5 us (2%)
  matrix products  11.3 us (2%)
    psum x1, waiting for transfers between devices, shards(): gram_total = lax.psum(local_gram, ('fib', 'blk'))  470 us
    all_to_all x1, blocking collectives, shards(): lax.all_to_all(field_data, 'fib', split_axis=3, concat_axis=2, tiled=True)  34.1 us
    unnamed x7, local copies, waits for them, and re-layouts  33.4 us
    all_to_all x3, local copies, waits for them, and re-layouts, shards(): lax.all_to_all(field_data, 'fib', split_axis=3, concat_axis=2, tiled=True)  18.9 us
    all_to_all x1, blocking collectives, shards(): lax.all_to_all(core_local, 'fib', split_axis=2, concat_axis=3, tiled=True)  14.6 us
  transfers between devices with their start and end apart: 1, of which 1 were waited for; matrix products, arithmetic and copies ran while one was open for 0% of the time, Pallas kernels for 0%

commit v1 on v0

--- a/solution.py
+++ b/solution.py
@@ -11,7 +11,7 @@
     unfolded = jnp.transpose(received, (0, 1, 3, 2)).reshape(-1, width_x)
     contract_rows = (((0,), (0,)), ((), ()))
     local_gram = lax.dot_general(unfolded, unfolded, contract_rows, precision=highest)
-    gram_total = lax.psum(local_gram, ("fib", "blk"))
+    gram_total = lax.psum(lax.psum(local_gram, "blk"), "fib")
     raw_basis = jnp.dot(gram_total, start_block, precision=highest)
     inner_block = jnp.dot(raw_basis.T, raw_basis, precision=highest)
     lower_factor = jnp.linalg.cholesky(inner_block)

time: 620 us -> 483 us (0.78)
  waiting for transfers between devices: 470 us -> 334 us
    psum x1 -> x2, waiting for transfers between devices: 470 us -> 334 us  [shards(): gram_total = lax.psum(lax.psum(local_gram, 'blk'), 'fib')]
  transfers between devices with their start and end apart: 1 -> 2, of which waited for: 1 -> 2; matrix products, arithmetic and copies ran while one was open for 0% -> 0% of each run, Pallas kernels for 0% -> 0%
where the time goes in v1:
time: 483 us; the launch traced here: 480 us
  waiting for transfers between devices  334 us (69%)
  local copies, waits for them, and re-layouts  54.5 us (11%)
  blocking collectives  45.9 us (10%)
  other arithmetic  20.9 us (4%)
  between operations  13.5 us (3%)
  matrix products  11.3 us (2%)
    psum x2, waiting for transfers between devices, shards(): gram_total = lax.psum(lax.psum(local_gram, 'blk'), 'fib')  334 us
    all_to_all x1, blocking collectives, shards(): lax.all_to_all(field_data, 'fib', split_axis=3, concat_axis=2, tiled=True)  34.1 us
    unnamed x7, local copies, waits for them, and re-layouts  33.4 us
    all_to_all x3, local copies, waits for them, and re-layouts, shards(): lax.all_to_all(field_data, 'fib', split_axis=3, concat_axis=2, tiled=True)  18.9 us
    all_to_all x1, blocking collectives, shards(): lax.all_to_all(core_local, 'fib', split_axis=2, concat_axis=3, tiled=True)  11.8 us
  transfers between devices with their start and end apart: 2, of which 2 were waited for; matrix products, arithmetic and copies ran while one was open for 0% of the time, Pallas kernels for 0%

profile of v1, /device:TPU:1, one launch (start us, length us, event | category | flops | bytes accessed | tf_op | source)
XLA Modules:
  0.0 480.0 jit_solution(11304184995907510564)
XLA Ops:
  6.5 0.0 copy-start
  6.5 0.0 all-reduce.3.cloned.1.call-start
  6.5 8.7 %copy.13 = f32[33,2,32,256]{0,2,1,3:T(8,128)} copy(f32[33,2,32,256]{3,2,1,0:T(8,128)} %param.2) | data formatting | bytes 4325376 | tf_op args[0]
  15.2 10.1 %reshape.13 = f32[16,1,33792]{2,1,0:T(1,128)S(1)} reshape(f32[256,2,32,33]{3,2,1,0:T(8,128)} %bitcast.45) | data formatting | bytes 4325376
  25.3 34.1 %all_to_all.36 = f32[16,1,33792]{2,1,0:T(1,128)} all-to-all(f32[16,1,33792]{2,1,0:T(1,128)S(1)} %reshape.13), channel_id=1, replica_groups=mesh['fib'=16,'blk'=32] {'fib'}, dimensions={0} | all-to-all | bytes 4325376 | tf_op jit(solution)/shard_map/all_to_all | solution.py:9
  59.4 0.5 broadcast.53
  59.9 7.4 %reduce.6 = f32[16,33792]{1,0:T(8,128)S(1)} reduce(f32[16,1,33792]{2,1,0:T(1,128)} %all_to_all.36, f32[]{:T(128)} %broadcast.53), dimensions={1}, to_apply=%all_to_all.26.reduce_sub_computation | reduce | bytes 4325380 | tf_op jit(solution)/shard_map/all_to_all | solution.py:9
  67.3 12.4 %reshape.14 = f32[256,2,32,33]{3,2,1,0:T(8,128)} reshape(f32[16,33792]{1,0:T(8,128)S(1)} %reduce.6) | data formatting | bytes 4325376
  79.8 11.7 %copy.15 = f32[33,2,16,32,16]{3,2,4,1,0:T(8,128)} copy(f32[33,2,16,32,16]{0,3,1,4,2:T(8,128)} %bitcast.46) | data formatting | bytes 4325376 | tf_op jit(solution)/shard_map/all_to_all | solution.py:9
  91.5 6.7 %all_to_all.29 = f32[33,2,512,16]{2,3,1,0:T(8,128)S(1)} reshape(f32[33,2,16,32,16]{3,2,4,1,0:T(8,128)} %copy.15) | data formatting | bytes 4325376 | tf_op jit(solution)/shard_map/all_to_all | solution.py:9
  98.2 5.4 %fusion.4 = f32[512,512]{1,0:T(8,128)} fusion(f32[33,2,512,16]{2,3,1,0:T(8,128)S(1)} %all_to_all.29), kind=kOutput, calls=%fused_computation.4 | convolution fusion | flops 3321888768 | bytes 3211264 | tf_op jit(solution)/shard_map/dot_general | solution.py:13
  103.5 0.0 all-reduce.3.cloned.1.call-update
  103.6 0.0 all-reduce.5.cloned.1.call-start
  103.6 214.2 %all-reduce.3.cloned.1.call-done = f32[512,512]{1,0:T(8,128)} async-done(((f32[512,512]{1,0:T(8,128)}), f32[512,512]{1,0:T(8,128)}) %all-reduce.3.cloned.1.call-update) | async-done | bytes 1048592 | tf_op jit(solution)/shard_map/psum | solution.py:14
  317.8 0.0 all-reduce.5.cloned.1.call-update
  317.8 119.6 %all-reduce.5.cloned.1.call-done = f32[512,512]{1,0:T(8,128)} async-done(((f32[512,512]{1,0:T(8,128)}), f32[512,512]{1,0:T(8,128)}) %all-reduce.5.cloned.1.call-update) | async-done | bytes 1048592 | tf_op jit(solution)/shard_map/psum | solution.py:14
  437.4 0.0 copy-done
  437.4 2.4 fusion.13
  439.8 0.3 fusion.14
  440.1 0.1 copy.16
  440.2 5.8 %cholesky.16 = f32[64,64]{1,0:T(8,128)S(1)} custom-call(f32[64,64]{1,0:T(8,128)S(1)} %fusion.12), custom_call_target="Cholesky" | custom-call | tf_op jit(solution)/shard_map/jit(cholesky)/cholesky | solution.py:17
  446.0 0.7 compare_reduce_fusion
  446.8 0.7 fusion.10
  447.5 4.9 %custom-call.7 = f32[1,64,64]{1,2,0:T(8,128)S(1)} custom-call(f32[1,64,64]{2,1,0:T(8,128)S(1)} %fusion.10), custom_call_target="InvertDiagBlocksLowerTriangular" | custom-call | tf_op jit(solution)/shard_map/jit(_solve_triangular)/triangular_solve | solution.py:18
  452.4 0.3 convolution_bitcast_fusion
  452.7 3.0 fusion.7
  455.7 1.0 copy.18
  456.7 1.0 reshape.15
  457.8 11.8 %all_to_all.37 = f32[16,1,4224]{2,1,0:T(1,128)S(1)} all-to-all(f32[16,1,4224]{2,1,0:T(1,128)S(1)} %reshape.15), channel_id=1, replica_groups=mesh['fib'=16,'blk'=32] {'fib'}, dimensions={0} | all-to-all | bytes 540672 | tf_op jit(solution)/shard_map/all_to_all | solution.py:20
  469.6 1.3 reduce.7
  470.8 1.1 reshape.16
  472.0 0.1 copy.20
  472.1 1.0 copy.21
  (2 shorter events, 0.0 us)
Async XLA Ops:
  6.5 430.9 %copy-start = (f32[512,64]{0,1:T(8,128)S(1)}, f32[512,64]{0,1:T(8,128)}, u32[]{:S(2)}) copy-start(f32[512,64]{0,1:T(8,128)} %param.3) | copy-start | bytes 393220
  6.5 311.3 %all-reduce.3.cloned.1.call-start = ((), (), s32[]{:S(2)}) async-start(), calls=%async_computation.2 | async-start | bytes 2097152 | tf_op jit(solution)/shard_map/psum | solution.py:14
  103.6 333.9 %all-reduce.5.cloned.1.call-start = ((), (), s32[]{:S(2)}) async-start(), calls=%async_computation.3 | async-start | bytes 2097152 | tf_op jit(solution)/shard_map/psum | solution.py:14
Sparse Core Ops, SparseCore 0:
  103.7 214.0 all-reduce.2
  321.4 116.0 all-reduce.4
